TPU v7x, 32 devices: a whole 2x2x4 slice. The times are simulated.
32 devices in a mesh: ctx: 4 (over y, x), grp: 4 (over z), side: 2 (over core).
Axes of the slice: x: 2, y: 2, z: 4, core: 2. Of those that a mesh axis runs over, the one named last changes fastest.
Arguments:
- tokens: bfloat16 [512, 2048], P(('ctx', 'grp', 'side')), may hold values from -6 to 6
- norm_gain: float32 [2048], replicated, may hold values from 0.25 to 1.75
- combine: float32 [512, 8], P(('ctx', 'grp', 'side')), may hold values from 0.05 to 0.6
- expert_ids: int32 [512, 8], P(('ctx', 'grp', 'side')), may hold values from 0 to 15, all different within a row; in each aligned block of 16 rows (0 to 15, 16 to 31, ...) at most 11 rows name the same one
- w_gate: bfloat16 [16, 2048, 768], P(('ctx', 'grp'), None, 'side'), may hold values from -0.125 to 0.125
- w_up: bfloat16 [16, 2048, 768], P(('ctx', 'grp'), None, 'side'), may hold values from -0.125 to 0.125
- w_down: bfloat16 [16, 768, 2048], P(('ctx', 'grp'), 'side'), may hold values from -0.21875 to 0.21875
- d_out: bfloat16 [512, 2048], P(('ctx', 'grp', 'side')), may hold values from -6 to 6
Outputs:
- mixed: bfloat16 [512, 2048], P(('ctx', 'grp', 'side'))
- d_tokens: bfloat16 [512, 2048], P(('ctx', 'grp', 'side'))
- d_gain: float32 [2048], replicated
- d_combine: float32 [512, 8], P(('ctx', 'grp', 'side'))
- d_w_gate: bfloat16 [16, 2048, 768], P(('ctx', 'grp'), None, 'side')
- d_w_up: bfloat16 [16, 2048, 768], P(('ctx', 'grp'), None, 'side')
- d_w_down: bfloat16 [16, 768, 2048], P(('ctx', 'grp'), 'side')
Inputs may be any that keep to these rules, and one draw needn't show every extreme that they name: `expert_ids`: each row names 8 different experts; among the 16 rows of one device no expert is named more than 11 times, and that bound is reached.
All inputs are finite; a program needn't handle non-finite values.
Results may differ from a plain program's by a relative error of at most 0.0072.
Values may be sent and summed in bfloat16 or wider, within the bound.
A program may use at most 128 MiB of HBM per device.

v0:
```python
import jax
import jax.numpy as jnp
from jax import lax
from jax.sharding import PartitionSpec as P

EPS = 1e-06


def expert_pass(rows, grads, gate_w, up_w, down_w):
    a_gate = jnp.dot(rows, gate_w, preferred_element_type=jnp.float32)
    a_up = jnp.dot(rows, up_w, preferred_element_type=jnp.float32)
    sigmoid_gate = jax.nn.sigmoid(a_gate)
    silu_gate = a_gate * sigmoid_gate
    hidden = (silu_gate * a_up).astype(jnp.bfloat16)
    output = jnp.dot(hidden, down_w, preferred_element_type=jnp.float32)
    d_hidden = lax.dot_general(
        grads, down_w, (((1,), (1,)), ((), ())), preferred_element_type=jnp.float32
    )
    d_up = (d_hidden * silu_gate).astype(jnp.bfloat16)
    d_gate = (d_hidden * a_up * sigmoid_gate * (1.0 + a_gate * (1.0 - sigmoid_gate))).astype(
        jnp.bfloat16
    )
    d_rows = lax.dot_general(
        d_gate, gate_w, (((1,), (1,)), ((), ())), preferred_element_type=jnp.float32
    )
    d_rows = d_rows + lax.dot_general(
        d_up, up_w, (((1,), (1,)), ((), ())), preferred_element_type=jnp.float32
    )
    g_gate = lax.dot_general(
        rows, d_gate, (((0,), (0,)), ((), ())), preferred_element_type=jnp.float32
    )
    g_up = lax.dot_general(rows, d_up, (((0,), (0,)), ((), ())), preferred_element_type=jnp.float32)
    g_down = lax.dot_general(
        hidden, grads, (((0,), (0,)), ((), ())), preferred_element_type=jnp.float32
    )
    return (output, d_rows, g_gate, g_up, g_down)


def local(tokens, norm_gain, combine, expert_ids, w_gate, w_up, w_down, d_out):
    count = tokens.shape[0]
    width = tokens.shape[1]
    chosen = expert_ids.shape[1]
    n_ctx = lax.axis_size("ctx")
    n_grp = lax.axis_size("grp")
    experts = n_ctx * n_grp
    slots = max(2, (4 * count * chosen + 3 * experts - 1) // (3 * experts))
    places = experts * slots
    x_float = tokens.astype(jnp.float32)
    inv_rms = lax.rsqrt(jnp.mean(x_float * x_float, axis=1, keepdims=True) + EPS)
    normed = (x_float * inv_rms * norm_gain).astype(jnp.bfloat16)
    grad_float = d_out.astype(jnp.float32)
    flat_ids = expert_ids.reshape(-1)
    onehot = (flat_ids[:, None] == jnp.arange(experts, dtype=jnp.int32)[None, :]).astype(jnp.int32)
    before = jnp.cumsum(onehot, axis=0) - onehot
    slot = jnp.sum(before * onehot, axis=1)
    target = flat_ids * slots + slot
    select = (target[:, None] == jnp.arange(places, dtype=jnp.int32)[None, :]).astype(jnp.float32)
    per_token = select.reshape(count, chosen, places)
    token_map = jnp.sum(per_token, axis=1).astype(jnp.bfloat16)
    weighted = jnp.sum(per_token * combine[:, :, None], axis=1)
    send_rows = lax.dot_general(
        token_map, normed, (((0,), (0,)), ((), ())), preferred_element_type=jnp.float32
    ).astype(jnp.bfloat16)
    send_grads = lax.dot_general(
        weighted,
        grad_float,
        (((0,), (0,)), ((), ())),
        precision=lax.Precision.HIGHEST,
        preferred_element_type=jnp.float32,
    ).astype(jnp.bfloat16)
    rows_in, grads_in = (
        lax.all_to_all(
            send_rows.reshape(experts, slots, width),
            ("ctx", "grp"),
            split_axis=0,
            concat_axis=0,
            tiled=True,
        ),
        lax.all_to_all(
            send_grads.reshape(experts, slots, width),
            ("ctx", "grp"),
            split_axis=0,
            concat_axis=0,
            tiled=True,
        ),
    )
    full_gate, full_up, full_down = (
        lax.all_gather(w_gate[0], "side", axis=1, tiled=True),
        lax.all_gather(w_up[0], "side", axis=1, tiled=True),
        lax.all_gather(w_down[0], "side", axis=0, tiled=True),
    )
    output, d_rows, g_gate, g_up, g_down = expert_pass(
        rows_in.reshape(places, width),
        grads_in.reshape(places, width),
        full_gate,
        full_up,
        full_down,
    )
    own_gate, own_up, own_down = (
        lax.psum_scatter(g_gate, "side", scatter_dimension=1, tiled=True),
        lax.psum_scatter(g_up, "side", scatter_dimension=1, tiled=True),
        lax.psum_scatter(g_down, "side", scatter_dimension=0, tiled=True),
    )
    back_out = output.astype(jnp.bfloat16)
    back_rows = d_rows.astype(jnp.bfloat16)
    came_out, came_rows = (
        lax.all_to_all(
            back_out.reshape(experts, slots, width),
            ("ctx", "grp"),
            split_axis=0,
            concat_axis=0,
            tiled=True,
        ),
        lax.all_to_all(
            back_rows.reshape(experts, slots, width),
            ("ctx", "grp"),
            split_axis=0,
            concat_axis=0,
            tiled=True,
        ),
    )
    slot_out = jnp.dot(
        select.astype(jnp.bfloat16),
        came_out.reshape(places, width),
        preferred_element_type=jnp.float32,
    ).reshape(count, chosen, width)
    mixed = (x_float + jnp.sum(combine[:, :, None] * slot_out, axis=1)).astype(jnp.bfloat16)
    d_combine = jnp.einsum("tkd,td->tk", slot_out, grad_float, precision=lax.Precision.HIGHEST)
    d_normed = jnp.dot(
        token_map, came_rows.reshape(places, width), preferred_element_type=jnp.float32
    )
    d_gain = lax.psum(jnp.sum(d_normed * x_float * inv_rms, axis=0), ("ctx", "grp", "side"))
    scaled = d_normed * norm_gain
    d_tokens = (
        grad_float
        + inv_rms * scaled
        - x_float * inv_rms**3 * jnp.mean(scaled * x_float, axis=1, keepdims=True)
    )
    return (
        mixed,
        d_tokens.astype(jnp.bfloat16),
        d_gain,
        d_combine,
        own_gate.astype(jnp.bfloat16)[None],
        own_up.astype(jnp.bfloat16)[None],
        own_down.astype(jnp.bfloat16)[None],
    )


def solution(mesh):
    in_specs = (
        P(("ctx", "grp", "side"), None),
        P(),
        P(("ctx", "grp", "side"), None),
        P(("ctx", "grp", "side"), None),
        P(("ctx", "grp"), None, "side"),
        P(("ctx", "grp"), None, "side"),
        P(("ctx", "grp"), "side", None),
        P(("ctx", "grp", "side"), None),
    )
    out_specs = (
        P(("ctx", "grp", "side"), None),
        P(("ctx", "grp", "side"), None),
        P(),
        P(("ctx", "grp", "side"), None),
        P(("ctx", "grp"), None, "side"),
        P(("ctx", "grp"), None, "side"),
        P(("ctx", "grp"), "side", None),
    )
    return jax.shard_map(local, mesh=mesh, in_specs=in_specs, out_specs=out_specs, check_vma=False)
```

profile of v0, /device:TPU:12, one launch (start us, length us, event | category | flops | bytes accessed | tf_op | source)
XLA Modules:
  0.0 222.5 jit_solution(12201147010498002594)
XLA Ops:
  7.2 0.7 all-gather.11.cloned.1.call-update
  8.0 0.7 all-gather.9.cloned.1.call-update
  8.7 0.1 copy.23
  8.8 0.1 eq.49
  8.9 0.1 fusion.41
  9.0 0.2 reduce_window_sum.11
  9.2 0.2 select_reduce_fusion.1
  9.4 0.1 reduce_sum.66
  9.5 0.2 select_reduce_fusion
  9.7 0.8 convolution_convert_fusion
  10.5 1.2 reshape.111
  11.7 7.2 %all-to-all-start.2 = ((bf16[16,11,2048]{2,1,0:T(8,128)(2,1)}), bf16[16,11,2048]{2,1,0:T(8,128)(2,1)S(1)}, u32[]{:S(2)}, u32[]{:S(2)}) async-start(bf16[16,11,2048]{2,1,0:T(8,128)(2,1)} %reshape.111), calls=%async_computation.2 | async-start | bytes 2097152 | tf_op jit(solution)/shard_map/all_to_all | solution.py:79
  18.9 0.7 all-gather.7.cloned.1.call-update
  19.6 0.1 fusion.22
  19.8 0.5 multiply_multiply_fusion
  20.3 0.4 convolution_convert_fusion.1
  20.7 1.2 reshape.107
  21.9 20.6 %all-to-all-done.2 = bf16[16,11,2048]{2,1,0:T(8,128)(2,1)S(1)} async-done(((bf16[16,11,2048]{2,1,0:T(8,128)(2,1)}), bf16[16,11,2048]{2,1,0:T(8,128)(2,1)S(1)}, u32[]{:S(2)}, u32[]{:S(2)}) %all-to-all-start.2) | async-done | bytes 720928 | tf_op jit(solution)/shard_map/all_to_all | solution.py:79
  42.5 7.5 %all-to-all-start = ((bf16[16,11,2048]{2,1,0:T(8,128)(2,1)}), bf16[16,11,2048]{2,1,0:T(8,128)(2,1)S(1)}, u32[]{:S(2)}, u32[]{:S(2)}) async-start(bf16[16,11,2048]{2,1,0:T(8,128)(2,1)} %reshape.107), calls=%async_computation | async-start | bytes 2097152 | tf_op jit(solution)/shard_map/all_to_all | solution.py:72
  50.0 0.3 reshape.112
  50.3 22.6 %all-to-all-done = bf16[16,11,2048]{2,1,0:T(8,128)(2,1)S(1)} async-done(((bf16[16,11,2048]{2,1,0:T(8,128)(2,1)}), bf16[16,11,2048]{2,1,0:T(8,128)(2,1)S(1)}, u32[]{:S(2)}, u32[]{:S(2)}) %all-to-all-start) | async-done | bytes 720928 | tf_op jit(solution)/shard_map/all_to_all | solution.py:72
  72.9 0.3 reshape.108
  73.2 3.1 %fusion = f32[176,768]{1,0:T(8,128)S(1)} fusion(bf16[176,2048]{1,0:T(8,128)(2,1)S(1)} %reshape.112, bf16[1,768,2048]{2,1,0:T(8,128)(2,1)} %all-gather.11.cloned.1.call-done), kind=kOutput, calls=%fused_computation | convolution fusion | flops 553648128 | bytes 4407296 | tf_op jit(solution)/shard_map/dot_general | solution.py:16
  76.4 2.6 %fusion.6 = f32[176,768]{1,0:T(8,128)S(1)} fusion(bf16[176,2048]{1,0:T(8,128)(2,1)S(1)} %reshape.108, bf16[1,2048,768]{2,1,0:T(8,128)(2,1)} %all-gather.9.cloned.1.call-done), kind=kOutput, calls=%fused_computation.6 | convolution fusion | flops 553648128 | bytes 4407296 | tf_op jit(solution)/shard_map/dot_general | solution.py:11
  79.0 2.8 %multiply_convert_fusion.1 = (bf16[176,768]{1,0:T(8,128)(2,1)S(1)}, bf16[176,768]{1,0:T(8,128)(2,1)S(1)}, bf16[176,768]{1,0:T(8,128)(2,1)S(1)}) fusion(f32[176,768]{1,0:T(8,128)S(1)} %fusion, f32[176,768]{1,0:T(8,128)S(1)} %fusion.6, bf16[176,2048]{1,0:T(8,128)(2,1)S(1)} %reshape.108, bf16[1,2048,768]{2,1,0:T(8,128)(2,1)} %all-gather.7.cloned.1.call-done), kind=kOutput, calls=%fused_computation.22 | convolution fusion | flops 555675648 | bytes 5758976 | tf_op jit(solution)/shard_map/dot_general | solution.py:10
  81.8 3.6 %fusion.47 = f32[768,2048]{1,0:T(8,128)} fusion(bf16[176,768]{1,0:T(8,128)(2,1)S(1)} %get-tuple-element.13, bf16[176,2048]{1,0:T(8,128)(2,1)S(1)} %reshape.112), kind=kOutput, calls=%fused_computation.66 | convolution fusion | flops 553648128 | bytes 7282688 | tf_op jit(solution)/shard_map/dot_general | solution.py:33
  85.5 3.7 %fusion.45 = f32[2048,768]{1,0:T(8,128)} fusion(bf16[176,2048]{1,0:T(8,128)(2,1)S(1)} %reshape.108, bf16[176,768]{1,0:T(8,128)(2,1)S(1)} %get-tuple-element.11), kind=kOutput, calls=%fused_computation.64 | convolution fusion | flops 553648128 | bytes 7282688 | tf_op jit(solution)/shard_map/dot_general | solution.py:29
  89.3 4.0 %fusion.46 = f32[2048,768]{1,0:T(8,128)} fusion(bf16[176,2048]{1,0:T(8,128)(2,1)S(1)} %reshape.108, bf16[176,768]{1,0:T(8,128)(2,1)S(1)} %get-tuple-element.12), kind=kOutput, calls=%fused_computation.65 | convolution fusion | flops 553648128 | bytes 7282688 | tf_op jit(solution)/shard_map/dot_general | solution.py:32
  93.4 3.7 %fusion.15 = bf16[176,2048]{1,0:T(8,128)(2,1)} fusion(bf16[176,768]{1,0:T(8,128)(2,1)S(1)} %get-tuple-element.13, bf16[1,768,2048]{2,1,0:T(8,128)(2,1)} %all-gather.11.cloned.1.call-done), kind=kOutput, calls=%fused_computation.13 | convolution fusion | flops 554008576 | bytes 4136960 | tf_op jit(solution)/shard_map/dot_general | solution.py:15
  97.1 2.6 %reshape.109 = bf16[16,11,2048]{2,1,0:T(8,128)(2,1)} reshape(bf16[176,2048]{1,0:T(8,128)(2,1)} %fusion.15) | data formatting | bytes 1441792 | tf_op jit(solution)/shard_map/reshape | solution.py:108
  99.6 9.3 %all-to-all-start.1 = ((bf16[16,11,2048]{2,1,0:T(8,128)(2,1)}), bf16[16,11,2048]{2,1,0:T(8,128)(2,1)}, u32[]{:S(2)}, u32[]{:S(2)}) async-start(bf16[16,11,2048]{2,1,0:T(8,128)(2,1)} %reshape.109), calls=%async_computation.1 | async-start | bytes 2097152 | tf_op jit(solution)/shard_map/all_to_all | solution.py:107
  108.9 2.3 %fusion.4 = f32[176,2048]{1,0:T(8,128)S(1)} fusion(bf16[176,768]{1,0:T(8,128)(2,1)} %copy-done.4, bf16[1,2048,768]{2,1,0:T(8,128)(2,1)S(1)} %copy-done), kind=kOutput, calls=%fused_computation.4 | convolution fusion | flops 553648128 | bytes 4857856 | tf_op jit(solution)/shard_map/dot_general | solution.py:26
  111.2 1.2 fusion.18
  112.4 1.2 reshape.113
  113.7 17.7 %all-to-all-done.1 = bf16[16,11,2048]{2,1,0:T(8,128)(2,1)} async-done(((bf16[16,11,2048]{2,1,0:T(8,128)(2,1)}), bf16[16,11,2048]{2,1,0:T(8,128)(2,1)}, u32[]{:S(2)}, u32[]{:S(2)}) %all-to-all-start.1) | async-done | bytes 720928 | tf_op jit(solution)/shard_map/all_to_all | solution.py:107
  131.4 7.5 %all-to-all-start.3 = ((bf16[16,11,2048]{2,1,0:T(8,128)(2,1)}), bf16[16,11,2048]{2,1,0:T(8,128)(2,1)S(1)}, u32[]{:S(2)}, u32[]{:S(2)}) async-start(bf16[16,11,2048]{2,1,0:T(8,128)(2,1)} %reshape.113), calls=%async_computation.3 | async-start | bytes 2097152 | tf_op jit(solution)/shard_map/all_to_all | solution.py:114
  138.9 1.5 reshape.118
  140.4 0.5 multiply_reduce_fusion
  140.9 1.1 fusion.32
  142.1 0.7 copy.28
  142.8 19.0 %all-to-all-done.3 = bf16[16,11,2048]{2,1,0:T(8,128)(2,1)S(1)} async-done(((bf16[16,11,2048]{2,1,0:T(8,128)(2,1)}), bf16[16,11,2048]{2,1,0:T(8,128)(2,1)S(1)}, u32[]{:S(2)}, u32[]{:S(2)}) %all-to-all-start.3) | async-done | bytes 720928 | tf_op jit(solution)/shard_map/all_to_all | solution.py:114
  161.8 0.3 reshape.114
  162.1 0.3 fusion.31
  162.4 42.8 %psum.7 = f32[2048]{0:T(1024)} all-reduce(f32[2048]{0:T(1024)S(1)} %get-tuple-element.7), channel_id=1, replica_groups=mesh['ctx'=4,'grp'=4,'side'=2] {'ctx','grp','side'}, use_global_device_ids=true, to_apply=%region_8.9 | all-reduce | flops 2048 | bytes 16384 | tf_op jit(solution)/shard_map/psum | solution.py:132
  205.2 0.7 fusion.28
  206.0 3.3 %convert_bitcast_fusion = bf16[1,384,2048]{2,1,0:T(8,128)(2,1)} fusion(f32[384,2048]{1,0:T(8,128)} %reduce-scatter.8.cloned.1.call-done), kind=kLoop, calls=%fused_computation.17 | loop fusion | flops 786432 | bytes 4718592 | tf_op jit(solution)/shard_map/broadcast_in_dim | solution.py:146
  209.2 3.2 %convert_bitcast_fusion.2 = bf16[1,2048,384]{2,1,0:T(8,128)(2,1)} fusion(f32[2048,384]{1,0:T(8,128)} %reduce-scatter.4.cloned.1.call-done), kind=kLoop, calls=%fused_computation.19 | loop fusion | flops 786432 | bytes 4718592 | tf_op jit(solution)/shard_map/broadcast_in_dim | solution.py:144
  212.4 3.2 %convert_bitcast_fusion.1 = bf16[1,2048,384]{2,1,0:T(8,128)(2,1)} fusion(f32[2048,384]{1,0:T(8,128)} %reduce-scatter.6.cloned.1.call-done), kind=kLoop, calls=%fused_computation.18 | loop fusion | flops 786432 | bytes 4718592 | tf_op jit(solution)/shard_map/broadcast_in_dim | solution.py:145
  (56 shorter events, 0.5 us)
Async XLA Ops:
  7.2 1.5 copy-start.16
  7.2 1.6 copy-start.17
  7.2 2.5 %copy-start.5 = (bf16[16,2048]{1,0:T(8,128)(2,1)S(1)}, bf16[16,2048]{1,0:T(8,128)(2,1)}, u32[]{:S(2)}) copy-start(bf16[16,2048]{1,0:T(8,128)(2,1)} %param.15) | copy-start | bytes 196612
  7.2 66.0 %all-gather.11.cloned.1.call-start = ((), (), s32[]{:S(2)}) async-start(), calls=%async_computation.12 | async-start | bytes 4718592 | tf_op jit(solution)/shard_map/all_gather | solution.py:90
  7.9 68.4 %all-gather.9.cloned.1.call-start = ((), (), s32[]{:S(2)}) async-start(), calls=%async_computation.11 | async-start | bytes 4718592 | tf_op jit(solution)/shard_map/all_gather | solution.py:89
  8.8 10.8 %copy-start.12 = (f32[16,8]{1,0:T(8,128)}, f32[16,8]{1,0:T(8,128)S(1)}, u32[]{:S(2)}) copy-start(f32[16,8]{1,0:T(8,128)S(1)} %copy.23) | copy-start | bytes 1540
  9.5 10.3 %copy-start.10 = (s32[16,8]{1,0:T(8,128)}, s32[16,8]{1,0:T(8,128)S(1)}, u32[]{:S(2)}) copy-start(s32[16,8]{1,0:T(8,128)S(1)} %multiply_add_fusion) | copy-start | bytes 1540
  9.5 10.1 %copy-start.6 = (bf16[16,2048]{1,0:T(8,128)(2,1)S(1)}, bf16[16,2048]{1,0:T(8,128)(2,1)}, u32[]{:S(2)}) copy-start(bf16[16,2048]{1,0:T(8,128)(2,1)} %param.8) | copy-start | bytes 196612
  9.7 10.6 %copy-start.8 = (bf16[16,176]{1,0:T(8,128)(2,1)}, bf16[16,176]{1,0:T(8,128)(2,1)S(1)}, u32[]{:S(2)}) copy-start(bf16[16,176]{1,0:T(8,128)(2,1)S(1)} %get-tuple-element.10) | copy-start | bytes 16900
  9.7 10.6 %copy-start.7 = (f32[2048]{0:T(1024)S(1)}, f32[2048]{0:T(1024)}, u32[]{:S(2)}) copy-start(f32[2048]{0:T(1024)} %param.9) | copy-start | bytes 24580
  11.7 30.8 %all-to-all-start.2 = ((bf16[16,11,2048]{2,1,0:T(8,128)(2,1)}), bf16[16,11,2048]{2,1,0:T(8,128)(2,1)S(1)}, u32[]{:S(2)}, u32[]{:S(2)}) async-start(bf16[16,11,2048]{2,1,0:T(8,128)(2,1)} %reshape.111), calls=%async_computation.2 | async-start | bytes 2097152 | tf_op jit(solution)/shard_map/all_to_all | solution.py:79
  18.9 60.1 %all-gather.7.cloned.1.call-start = ((), (), s32[]{:S(2)}) async-start(), calls=%async_computation.10 | async-start | bytes 4718592 | tf_op jit(solution)/shard_map/all_gather | solution.py:88
  20.3 22.2 %copy-start.14 = (f32[16]{0:T(128)}, f32[16]{0:T(128)S(1)}, u32[]{:S(2)}) copy-start(f32[16]{0:T(128)S(1)} %get-tuple-element.17) | copy-start | bytes 196
  42.5 30.5 %all-to-all-start = ((bf16[16,11,2048]{2,1,0:T(8,128)(2,1)}), bf16[16,11,2048]{2,1,0:T(8,128)(2,1)S(1)}, u32[]{:S(2)}, u32[]{:S(2)}) async-start(bf16[16,11,2048]{2,1,0:T(8,128)(2,1)} %reshape.107), calls=%async_computation | async-start | bytes 2097152 | tf_op jit(solution)/shard_map/all_to_all | solution.py:72
  49.9 156.0 %reduce-scatter.8.cloned.1.call-start = ((), (), s32[]{:S(2)}) async-start(), calls=%async_computation.9 | async-start | bytes 9437184 | tf_op jit(solution)/shard_map/reduce_scatter | solution.py:102
  81.8 3.7 %copy-start.2 = (bf16[176,768]{1,0:T(8,128)(2,1)}, bf16[176,768]{1,0:T(8,128)(2,1)S(1)}, u32[]{:S(2)}) copy-start(bf16[176,768]{1,0:T(8,128)(2,1)S(1)} %get-tuple-element.11) | copy-start | bytes 811012
  81.8 7.5 %copy-start.4 = (bf16[176,768]{1,0:T(8,128)(2,1)}, bf16[176,768]{1,0:T(8,128)(2,1)S(1)}, u32[]{:S(2)}) copy-start(bf16[176,768]{1,0:T(8,128)(2,1)S(1)} %get-tuple-element.12) | copy-start | bytes 811012
  85.5 123.8 %reduce-scatter.4.cloned.1.call-start = ((), (), s32[]{:S(2)}) async-start(), calls=%async_computation.7 | async-start | bytes 9437184 | tf_op jit(solution)/shard_map/reduce_scatter | solution.py:100
  89.3 123.2 %reduce-scatter.6.cloned.1.call-start = ((), (), s32[]{:S(2)}) async-start(), calls=%async_computation.8 | async-start | bytes 9437184 | tf_op jit(solution)/shard_map/reduce_scatter | solution.py:101
  93.3 15.6 %copy-start = (bf16[1,2048,768]{2,1,0:T(8,128)(2,1)S(1)}, bf16[1,2048,768]{2,1,0:T(8,128)(2,1)}, u32[]{:S(2)}) copy-start(bf16[1,2048,768]{2,1,0:T(8,128)(2,1)} %all-gather.9.cloned.1.call-done) | copy-start | bytes 9437188
  99.6 11.6 %copy-start.3 = (bf16[176,768]{1,0:T(8,128)(2,1)S(1)}, bf16[176,768]{1,0:T(8,128)(2,1)}, u32[]{:S(2)}) copy-start(bf16[176,768]{1,0:T(8,128)(2,1)} %copy-done.2) | copy-start | bytes 811012
  99.6 31.8 %all-to-all-start.1 = ((bf16[16,11,2048]{2,1,0:T(8,128)(2,1)}), bf16[16,11,2048]{2,1,0:T(8,128)(2,1)}, u32[]{:S(2)}, u32[]{:S(2)}) async-start(bf16[16,11,2048]{2,1,0:T(8,128)(2,1)} %reshape.109), calls=%async_computation.1 | async-start | bytes 2097152 | tf_op jit(solution)/shard_map/all_to_all | solution.py:107
  108.9 2.3 %copy-start.1 = (bf16[1,2048,768]{2,1,0:T(8,128)(2,1)S(1)}, bf16[1,2048,768]{2,1,0:T(8,128)(2,1)}, u32[]{:S(2)}) copy-start(bf16[1,2048,768]{2,1,0:T(8,128)(2,1)} %all-gather.7.cloned.1.call-done) | copy-start | bytes 9437188
  112.4 28.0 %copy-start.11 = (s32[16,8]{1,0:T(8,128)S(1)}, s32[16,8]{1,0:T(8,128)}, u32[]{:S(2)}) copy-start(s32[16,8]{1,0:T(8,128)} %copy-done.10) | copy-start | bytes 1540
  112.4 28.0 %copy-start.13 = (f32[16,8]{1,0:T(8,128)S(1)}, f32[16,8]{1,0:T(8,128)}, u32[]{:S(2)}) copy-start(f32[16,8]{1,0:T(8,128)} %copy-done.12) | copy-start | bytes 1540
  131.4 30.4 %all-to-all-start.3 = ((bf16[16,11,2048]{2,1,0:T(8,128)(2,1)}), bf16[16,11,2048]{2,1,0:T(8,128)(2,1)S(1)}, u32[]{:S(2)}, u32[]{:S(2)}) async-start(bf16[16,11,2048]{2,1,0:T(8,128)(2,1)} %reshape.113), calls=%async_computation.3 | async-start | bytes 2097152 | tf_op jit(solution)/shard_map/all_to_all | solution.py:114
  138.9 23.2 %copy-start.9 = (bf16[16,176]{1,0:T(8,128)(2,1)S(1)}, bf16[16,176]{1,0:T(8,128)(2,1)}, u32[]{:S(2)}) copy-start(bf16[16,176]{1,0:T(8,128)(2,1)} %copy-done.8) | copy-start | bytes 16900
  138.9 23.2 %copy-start.15 = (f32[16]{0:T(128)S(1)}, f32[16]{0:T(128)}, u32[]{:S(2)}) copy-start(f32[16]{0:T(128)} %copy-done.14) | copy-start | bytes 196
  140.4 64.8 %copy-start.18 = (f32[16]{0:T(128)S(1)}, f32[16]{0:T(128)}, u32[]{:S(2)}) copy-start(f32[16]{0:T(128)} %get-tuple-element.16) | copy-start | bytes 196
Sparse Core Ops, SparseCore 0:
  9.6 13.4 all-gather.10
  24.6 13.1 all-gather.8
  39.4 13.1 all-gather.6
  85.6 15.8 reduce-scatter.7
  103.6 15.1 reduce-scatter.3
  120.9 15.0 reduce-scatter.5
where the time goes:
time: 223 us; the launch traced here: 222 us
  waiting for transfers between devices  82.1 us (37%)
  blocking collectives  42.8 us (19%)
  starting transfers between devices  31.6 us (14%)
  matrix products  30.1 us (13%)
  between operations  14.5 us (7%)
  other arithmetic  11.7 us (5%)
  local copies, waits for them, and re-layouts  9.69 us (4%)
    psum x1, blocking collectives, local(): lax.psum(jnp.sum(d_normed * x_float * inv_rms, axis=0), ('ctx', 'grp', 's...  42.8 us
    all_to_all x1, waiting for transfers between devices, local(): lax.all_to_all(send_rows.reshape(experts, slots, width), ('ctx', 'grp'),...  22.6 us
    all_to_all x1, waiting for transfers between devices, local(): lax.all_to_all(send_grads.reshape(experts, slots, width), ('ctx', 'grp'),...  20.6 us
    all_to_all x1, waiting for transfers between devices, local(): lax.all_to_all(back_rows.reshape(experts, slots, width), ('ctx', 'grp'),...  19 us
    all_to_all x1, waiting for transfers between devices, local(): lax.all_to_all(back_out.reshape(experts, slots, width), ('ctx', 'grp'), s...  17.7 us
    all_to_all x1, starting transfers between devices, local(): lax.all_to_all(back_out.reshape(experts, slots, width), ('ctx', 'grp'), s...  9.28 us
    all_to_all x1, starting transfers between devices, local(): lax.all_to_all(back_rows.reshape(experts, slots, width), ('ctx', 'grp'),...  7.49 us
    all_to_all x1, starting transfers between devices, local(): lax.all_to_all(send_rows.reshape(experts, slots, width), ('ctx', 'grp'),...  7.48 us
  transfers between devices with their start and end apart: 10, of which 4 were waited for; matrix products, arithmetic and copies ran while one was open for 19% of the time, Pallas kernels for 0%

commit v1 on v0

--- a/solution.py
+++ b/solution.py
@@ -2,6 +2,7 @@
 import jax.numpy as jnp
 from jax import lax
 from jax.sharding import PartitionSpec as P
+from jax.lax import psum
 
 EPS = 1e-06
 
@@ -129,7 +130,9 @@
     d_normed = jnp.dot(
         token_map, came_rows.reshape(places, width), preferred_element_type=jnp.float32
     )
-    d_gain = lax.psum(jnp.sum(d_normed * x_float * inv_rms, axis=0), ("ctx", "grp", "side"))
+    local_x = jnp.sum(d_normed * x_float * inv_rms, axis=0)
+    b_next = psum(local_x, axis_name="ctx")
+    d_gain = psum(b_next, ("grp", "side"))
     scaled = d_normed * norm_gain
     d_tokens = (
         grad_float

time: 223 us -> 208 us (0.933)
  the two profiles are of different devices: /device:TPU:12 before, /device:TPU:0 now
where the time goes in v1:
time: 208 us; the launch traced here: 207 us
  waiting for transfers between devices  97.1 us (47%)
  matrix products  31.4 us (15%)
  blocking collectives  22.7 us (11%)
  starting transfers between devices  20.6 us (10%)
  between operations  14.5 us (7%)
  other arithmetic  11.7 us (6%)
  local copies, waits for them, and re-layouts  9.45 us (5%)
    all_to_all x1, waiting for transfers between devices, local(): lax.all_to_all(send_rows.reshape(experts, slots, width), ('ctx', 'grp'),...  26.4 us
    all_to_all x1, waiting for transfers between devices, local(): lax.all_to_all(send_grads.reshape(experts, slots, width), ('ctx', 'grp'),...  24.4 us
    all_to_all x1, waiting for transfers between devices, local(): lax.all_to_all(back_rows.reshape(experts, slots, width), ('ctx', 'grp'),...  22.6 us
    all_to_all x1, waiting for transfers between devices, local(): lax.all_to_all(back_out.reshape(experts, slots, width), ('ctx', 'grp'), s...  21.5 us
    psum x1, blocking collectives, local(): d_gain = psum(b_next, ('grp', 'side'))  14.5 us
    all_to_all x1, starting transfers between devices, local(): lax.all_to_all(send_grads.reshape(experts, slots, width), ('ctx', 'grp'),...  8.34 us
    psum x1, blocking collectives, local(): b_next = psum(local_x, axis_name='ctx')  8.15 us
    dot_general x1, matrix products, expert_pass(): lax.dot_general(rows, d_up, (((0,), (0,)), ((), ())), preferred_element_t...  4.81 us
  transfers between devices with their start and end apart: 10, of which 4 were waited for; matrix products, arithmetic and copies ran while one was open for 21% of the time, Pallas kernels for 0%

profile of v1, /device:TPU:0, one launch (start us, length us, event | category | flops | bytes accessed | tf_op | source)
XLA Modules:
  0.0 207.3 jit_solution(8917621593842196652)
XLA Ops:
  7.2 0.7 all-gather.11.cloned.1.call-update
  8.0 0.7 all-gather.9.cloned.1.call-update
  8.8 0.1 eq.49
  8.9 0.1 fusion.41
  9.0 0.2 reduce_window_sum.11
  9.2 0.2 select_reduce_fusion.1
  9.4 0.1 reduce_sum.66
  9.5 0.2 select_reduce_fusion
  9.7 0.8 convolution_convert_fusion
  10.5 1.2 reshape.111
  11.7 8.3 %all-to-all-start.2 = ((bf16[16,11,2048]{2,1,0:T(8,128)(2,1)}), bf16[16,11,2048]{2,1,0:T(8,128)(2,1)S(1)}, u32[]{:S(2)}, u32[]{:S(2)}) async-start(bf16[16,11,2048]{2,1,0:T(8,128)(2,1)} %reshape.111), calls=%async_computation.2 | async-start | bytes 2097152 | tf_op jit(solution)/shard_map/all_to_all | solution.py:80
  20.1 0.7 all-gather.7.cloned.1.call-update
  20.8 0.1 fusion.22
  20.9 0.6 multiply_multiply_fusion
  21.5 0.4 convolution_convert_fusion.1
  21.9 1.2 reshape.107
  23.2 24.4 %all-to-all-done.2 = bf16[16,11,2048]{2,1,0:T(8,128)(2,1)S(1)} async-done(((bf16[16,11,2048]{2,1,0:T(8,128)(2,1)}), bf16[16,11,2048]{2,1,0:T(8,128)(2,1)S(1)}, u32[]{:S(2)}, u32[]{:S(2)}) %all-to-all-start.2) | async-done | bytes 720928 | tf_op jit(solution)/shard_map/all_to_all | solution.py:80
  47.5 3.7 %all-to-all-start = ((bf16[16,11,2048]{2,1,0:T(8,128)(2,1)}), bf16[16,11,2048]{2,1,0:T(8,128)(2,1)S(1)}, u32[]{:S(2)}, u32[]{:S(2)}) async-start(bf16[16,11,2048]{2,1,0:T(8,128)(2,1)} %reshape.107), calls=%async_computation | async-start | bytes 2097152 | tf_op jit(solution)/shard_map/all_to_all | solution.py:73
  51.2 0.3 reshape.112
  51.5 26.4 %all-to-all-done = bf16[16,11,2048]{2,1,0:T(8,128)(2,1)S(1)} async-done(((bf16[16,11,2048]{2,1,0:T(8,128)(2,1)}), bf16[16,11,2048]{2,1,0:T(8,128)(2,1)S(1)}, u32[]{:S(2)}, u32[]{:S(2)}) %all-to-all-start) | async-done | bytes 720928 | tf_op jit(solution)/shard_map/all_to_all | solution.py:73
  78.0 0.3 reshape.108
  78.3 3.1 %fusion = f32[176,768]{1,0:T(8,128)S(1)} fusion(bf16[176,2048]{1,0:T(8,128)(2,1)S(1)} %reshape.112, bf16[1,768,2048]{2,1,0:T(8,128)(2,1)} %all-gather.11.cloned.1.call-done), kind=kOutput, calls=%fused_computation | convolution fusion | flops 553648128 | bytes 4407296 | tf_op jit(solution)/shard_map/dot_general | solution.py:17
  81.4 2.6 %fusion.6 = f32[176,768]{1,0:T(8,128)S(1)} fusion(bf16[176,2048]{1,0:T(8,128)(2,1)S(1)} %reshape.108, bf16[1,2048,768]{2,1,0:T(8,128)(2,1)} %all-gather.9.cloned.1.call-done), kind=kOutput, calls=%fused_computation.6 | convolution fusion | flops 553648128 | bytes 4407296 | tf_op jit(solution)/shard_map/dot_general | solution.py:12
  84.1 2.8 %multiply_convert_fusion.1 = (bf16[176,768]{1,0:T(8,128)(2,1)S(1)}, bf16[176,768]{1,0:T(8,128)(2,1)S(1)}, bf16[176,768]{1,0:T(8,128)(2,1)S(1)}) fusion(f32[176,768]{1,0:T(8,128)S(1)} %fusion, f32[176,768]{1,0:T(8,128)S(1)} %fusion.6, bf16[176,2048]{1,0:T(8,128)(2,1)S(1)} %reshape.108, bf16[1,2048,768]{2,1,0:T(8,128)(2,1)} %all-gather.7.cloned.1.call-done), kind=kOutput, calls=%fused_computation.22 | convolution fusion | flops 555675648 | bytes 5758976 | tf_op jit(solution)/shard_map/dot_general | solution.py:11
  86.9 3.6 %fusion.47 = f32[768,2048]{1,0:T(8,128)} fusion(bf16[176,768]{1,0:T(8,128)(2,1)S(1)} %get-tuple-element.13, bf16[176,2048]{1,0:T(8,128)(2,1)S(1)} %reshape.112), kind=kOutput, calls=%fused_computation.66 | convolution fusion | flops 553648128 | bytes 7282688 | tf_op jit(solution)/shard_map/dot_general | solution.py:34
  90.6 4.0 %fusion.45 = f32[2048,768]{1,0:T(8,128)} fusion(bf16[176,2048]{1,0:T(8,128)(2,1)S(1)} %reshape.108, bf16[176,768]{1,0:T(8,128)(2,1)S(1)} %get-tuple-element.11), kind=kOutput, calls=%fused_computation.64 | convolution fusion | flops 553648128 | bytes 7282688 | tf_op jit(solution)/shard_map/dot_general | solution.py:30
  94.7 4.8 %fusion.46 = f32[2048,768]{1,0:T(8,128)} fusion(bf16[176,2048]{1,0:T(8,128)(2,1)S(1)} %reshape.108, bf16[176,768]{1,0:T(8,128)(2,1)S(1)} %get-tuple-element.12), kind=kOutput, calls=%fused_computation.65 | convolution fusion | flops 553648128 | bytes 7282688 | tf_op jit(solution)/shard_map/dot_general | solution.py:33
  99.5 3.9 %fusion.15 = bf16[176,2048]{1,0:T(8,128)(2,1)} fusion(bf16[176,768]{1,0:T(8,128)(2,1)S(1)} %get-tuple-element.13, bf16[1,768,2048]{2,1,0:T(8,128)(2,1)} %all-gather.11.cloned.1.call-done), kind=kOutput, calls=%fused_computation.13 | convolution fusion | flops 554008576 | bytes 4136960 | tf_op jit(solution)/shard_map/dot_general | solution.py:16
  103.4 2.3 %reshape.109 = bf16[16,11,2048]{2,1,0:T(8,128)(2,1)} reshape(bf16[176,2048]{1,0:T(8,128)(2,1)} %fusion.15) | data formatting | bytes 1441792 | tf_op jit(solution)/shard_map/reshape | solution.py:109
  105.7 4.5 %all-to-all-start.1 = ((bf16[16,11,2048]{2,1,0:T(8,128)(2,1)}), bf16[16,11,2048]{2,1,0:T(8,128)(2,1)}, u32[]{:S(2)}, u32[]{:S(2)}) async-start(bf16[16,11,2048]{2,1,0:T(8,128)(2,1)} %reshape.109), calls=%async_computation.1 | async-start | bytes 2097152 | tf_op jit(solution)/shard_map/all_to_all | solution.py:108
  110.2 2.3 %fusion.4 = f32[176,2048]{1,0:T(8,128)S(1)} fusion(bf16[176,768]{1,0:T(8,128)(2,1)} %copy-done.4, bf16[1,2048,768]{2,1,0:T(8,128)(2,1)S(1)} %copy-done), kind=kOutput, calls=%fused_computation.4 | convolution fusion | flops 553648128 | bytes 4857856 | tf_op jit(solution)/shard_map/dot_general | solution.py:27
  112.5 1.2 fusion.18
  113.7 1.2 reshape.113
  115.0 21.5 %all-to-all-done.1 = bf16[16,11,2048]{2,1,0:T(8,128)(2,1)} async-done(((bf16[16,11,2048]{2,1,0:T(8,128)(2,1)}), bf16[16,11,2048]{2,1,0:T(8,128)(2,1)}, u32[]{:S(2)}, u32[]{:S(2)}) %all-to-all-start.1) | async-done | bytes 720928 | tf_op jit(solution)/shard_map/all_to_all | solution.py:108
  136.4 3.8 %all-to-all-start.3 = ((bf16[16,11,2048]{2,1,0:T(8,128)(2,1)}), bf16[16,11,2048]{2,1,0:T(8,128)(2,1)S(1)}, u32[]{:S(2)}, u32[]{:S(2)}) async-start(bf16[16,11,2048]{2,1,0:T(8,128)(2,1)} %reshape.113), calls=%async_computation.3 | async-start | bytes 2097152 | tf_op jit(solution)/shard_map/all_to_all | solution.py:115
  140.3 1.5 reshape.118
  141.8 0.5 multiply_reduce_fusion
  142.3 1.1 fusion.32
  143.5 0.7 copy.28
  144.2 22.6 %all-to-all-done.3 = bf16[16,11,2048]{2,1,0:T(8,128)(2,1)S(1)} async-done(((bf16[16,11,2048]{2,1,0:T(8,128)(2,1)}), bf16[16,11,2048]{2,1,0:T(8,128)(2,1)S(1)}, u32[]{:S(2)}, u32[]{:S(2)}) %all-to-all-start.3) | async-done | bytes 720928 | tf_op jit(solution)/shard_map/all_to_all | solution.py:115
  166.8 0.3 reshape.114
  167.1 0.3 fusion.31
  167.4 8.2 %psum.14 = f32[2048]{0:T(1024)S(1)} all-reduce(f32[2048]{0:T(1024)S(1)} %get-tuple-element.7), channel_id=1, replica_groups=mesh['ctx'=4,'grp'=4,'side'=2] {'ctx'}, use_global_device_ids=true, to_apply=%region_8.9 | all-reduce | flops 2048 | bytes 16384 | tf_op jit(solution)/shard_map/psum | solution.py:134
  175.6 14.5 %psum.15 = f32[2048]{0:T(1024)} all-reduce(f32[2048]{0:T(1024)S(1)} %psum.14), channel_id=1, replica_groups=mesh['ctx'=4,'grp'=4,'side'=2] {'grp','side'}, use_global_device_ids=true, to_apply=%region_9.10 | all-reduce | flops 2048 | bytes 16384 | tf_op jit(solution)/shard_map/psum | solution.py:135
  190.1 0.7 fusion.28
  190.8 3.3 %convert_bitcast_fusion = bf16[1,384,2048]{2,1,0:T(8,128)(2,1)} fusion(f32[384,2048]{1,0:T(8,128)} %reduce-scatter.8.cloned.1.call-done), kind=kLoop, calls=%fused_computation.17 | loop fusion | flops 786432 | bytes 4718592 | tf_op jit(solution)/shard_map/broadcast_in_dim | solution.py:149
  194.1 3.2 %convert_bitcast_fusion.2 = bf16[1,2048,384]{2,1,0:T(8,128)(2,1)} fusion(f32[2048,384]{1,0:T(8,128)} %reduce-scatter.4.cloned.1.call-done), kind=kLoop, calls=%fused_computation.19 | loop fusion | flops 786432 | bytes 4718592 | tf_op jit(solution)/shard_map/broadcast_in_dim | solution.py:147
  197.3 3.2 %convert_bitcast_fusion.1 = bf16[1,2048,384]{2,1,0:T(8,128)(2,1)} fusion(f32[2048,384]{1,0:T(8,128)} %reduce-scatter.6.cloned.1.call-done), kind=kLoop, calls=%fused_computation.18 | loop fusion | flops 786432 | bytes 4718592 | tf_op jit(solution)/shard_map/broadcast_in_dim | solution.py:148
  (57 shorter events, 0.6 us)
Async XLA Ops:
  7.2 1.5 copy-start.16
  7.2 1.6 copy-start.17
  7.2 2.5 %copy-start.5 = (bf16[16,2048]{1,0:T(8,128)(2,1)S(1)}, bf16[16,2048]{1,0:T(8,128)(2,1)}, u32[]{:S(2)}) copy-start(bf16[16,2048]{1,0:T(8,128)(2,1)} %param.15) | copy-start | bytes 196612
  7.2 71.1 %all-gather.11.cloned.1.call-start = ((), (), s32[]{:S(2)}) async-start(), calls=%async_computation.12 | async-start | bytes 4718592 | tf_op jit(solution)/shard_map/all_gather | solution.py:91
  7.9 73.5 %all-gather.9.cloned.1.call-start = ((), (), s32[]{:S(2)}) async-start(), calls=%async_computation.11 | async-start | bytes 4718592 | tf_op jit(solution)/shard_map/all_gather | solution.py:90
  8.8 12.0 %copy-start.12 = (f32[16,8]{1,0:T(8,128)}, f32[16,8]{1,0:T(8,128)S(1)}, u32[]{:S(2)}) copy-start(f32[16,8]{1,0:T(8,128)S(1)} %copy.23) | copy-start | bytes 1540
  9.5 11.5 %copy-start.10 = (s32[16,8]{1,0:T(8,128)}, s32[16,8]{1,0:T(8,128)S(1)}, u32[]{:S(2)}) copy-start(s32[16,8]{1,0:T(8,128)S(1)} %multiply_add_fusion) | copy-start | bytes 1540
  9.5 11.3 %copy-start.6 = (bf16[16,2048]{1,0:T(8,128)(2,1)S(1)}, bf16[16,2048]{1,0:T(8,128)(2,1)}, u32[]{:S(2)}) copy-start(bf16[16,2048]{1,0:T(8,128)(2,1)} %param.8) | copy-start | bytes 196612
  9.7 11.9 %copy-start.8 = (bf16[16,176]{1,0:T(8,128)(2,1)}, bf16[16,176]{1,0:T(8,128)(2,1)S(1)}, u32[]{:S(2)}) copy-start(bf16[16,176]{1,0:T(8,128)(2,1)S(1)} %get-tuple-element.10) | copy-start | bytes 16900
  9.7 11.8 %copy-start.7 = (f32[2048]{0:T(1024)S(1)}, f32[2048]{0:T(1024)}, u32[]{:S(2)}) copy-start(f32[2048]{0:T(1024)} %param.9) | copy-start | bytes 24580
  11.7 35.8 %all-to-all-start.2 = ((bf16[16,11,2048]{2,1,0:T(8,128)(2,1)}), bf16[16,11,2048]{2,1,0:T(8,128)(2,1)S(1)}, u32[]{:S(2)}, u32[]{:S(2)}) async-start(bf16[16,11,2048]{2,1,0:T(8,128)(2,1)} %reshape.111), calls=%async_computation.2 | async-start | bytes 2097152 | tf_op jit(solution)/shard_map/all_to_all | solution.py:80
  20.0 64.0 %all-gather.7.cloned.1.call-start = ((), (), s32[]{:S(2)}) async-start(), calls=%async_computation.10 | async-start | bytes 4718592 | tf_op jit(solution)/shard_map/all_gather | solution.py:89
  21.5 26.0 %copy-start.14 = (f32[16]{0:T(128)}, f32[16]{0:T(128)S(1)}, u32[]{:S(2)}) copy-start(f32[16]{0:T(128)S(1)} %get-tuple-element.17) | copy-start | bytes 196
  47.5 30.5 %all-to-all-start = ((bf16[16,11,2048]{2,1,0:T(8,128)(2,1)}), bf16[16,11,2048]{2,1,0:T(8,128)(2,1)S(1)}, u32[]{:S(2)}, u32[]{:S(2)}) async-start(bf16[16,11,2048]{2,1,0:T(8,128)(2,1)} %reshape.107), calls=%async_computation | async-start | bytes 2097152 | tf_op jit(solution)/shard_map/all_to_all | solution.py:73
  51.2 139.6 %reduce-scatter.8.cloned.1.call-start = ((), (), s32[]{:S(2)}) async-start(), calls=%async_computation.9 | async-start | bytes 9437184 | tf_op jit(solution)/shard_map/reduce_scatter | solution.py:103
  86.9 3.7 %copy-start.2 = (bf16[176,768]{1,0:T(8,128)(2,1)}, bf16[176,768]{1,0:T(8,128)(2,1)S(1)}, u32[]{:S(2)}) copy-start(bf16[176,768]{1,0:T(8,128)(2,1)S(1)} %get-tuple-element.11) | copy-start | bytes 811012
  86.9 7.8 %copy-start.4 = (bf16[176,768]{1,0:T(8,128)(2,1)}, bf16[176,768]{1,0:T(8,128)(2,1)S(1)}, u32[]{:S(2)}) copy-start(bf16[176,768]{1,0:T(8,128)(2,1)S(1)} %get-tuple-element.12) | copy-start | bytes 811012
  90.5 103.6 %reduce-scatter.4.cloned.1.call-start = ((), (), s32[]{:S(2)}) async-start(), calls=%async_computation.7 | async-start | bytes 9437184 | tf_op jit(solution)/shard_map/reduce_scatter | solution.py:101
  94.6 102.7 %reduce-scatter.6.cloned.1.call-start = ((), (), s32[]{:S(2)}) async-start(), calls=%async_computation.8 | async-start | bytes 9437184 | tf_op jit(solution)/shard_map/reduce_scatter | solution.py:102
  99.5 10.7 %copy-start = (bf16[1,2048,768]{2,1,0:T(8,128)(2,1)S(1)}, bf16[1,2048,768]{2,1,0:T(8,128)(2,1)}, u32[]{:S(2)}) copy-start(bf16[1,2048,768]{2,1,0:T(8,128)(2,1)} %all-gather.9.cloned.1.call-done) | copy-start | bytes 9437188
  105.7 6.8 %copy-start.3 = (bf16[176,768]{1,0:T(8,128)(2,1)S(1)}, bf16[176,768]{1,0:T(8,128)(2,1)}, u32[]{:S(2)}) copy-start(bf16[176,768]{1,0:T(8,128)(2,1)} %copy-done.2) | copy-start | bytes 811012
  105.7 30.7 %all-to-all-start.1 = ((bf16[16,11,2048]{2,1,0:T(8,128)(2,1)}), bf16[16,11,2048]{2,1,0:T(8,128)(2,1)}, u32[]{:S(2)}, u32[]{:S(2)}) async-start(bf16[16,11,2048]{2,1,0:T(8,128)(2,1)} %reshape.109), calls=%async_computation.1 | async-start | bytes 2097152 | tf_op jit(solution)/shard_map/all_to_all | solution.py:108
  110.2 2.3 %copy-start.1 = (bf16[1,2048,768]{2,1,0:T(8,128)(2,1)S(1)}, bf16[1,2048,768]{2,1,0:T(8,128)(2,1)}, u32[]{:S(2)}) copy-start(bf16[1,2048,768]{2,1,0:T(8,128)(2,1)} %all-gather.7.cloned.1.call-done) | copy-start | bytes 9437188
  113.7 28.1 %copy-start.11 = (s32[16,8]{1,0:T(8,128)S(1)}, s32[16,8]{1,0:T(8,128)}, u32[]{:S(2)}) copy-start(s32[16,8]{1,0:T(8,128)} %copy-done.10) | copy-start | bytes 1540
  113.7 28.1 %copy-start.13 = (f32[16,8]{1,0:T(8,128)S(1)}, f32[16,8]{1,0:T(8,128)}, u32[]{:S(2)}) copy-start(f32[16,8]{1,0:T(8,128)} %copy-done.12) | copy-start | bytes 1540
  136.4 30.4 %all-to-all-start.3 = ((bf16[16,11,2048]{2,1,0:T(8,128)(2,1)}), bf16[16,11,2048]{2,1,0:T(8,128)(2,1)S(1)}, u32[]{:S(2)}, u32[]{:S(2)}) async-start(bf16[16,11,2048]{2,1,0:T(8,128)(2,1)} %reshape.113), calls=%async_computation.3 | async-start | bytes 2097152 | tf_op jit(solution)/shard_map/all_to_all | solution.py:115
  140.3 26.8 %copy-start.9 = (bf16[16,176]{1,0:T(8,128)(2,1)S(1)}, bf16[16,176]{1,0:T(8,128)(2,1)}, u32[]{:S(2)}) copy-start(bf16[16,176]{1,0:T(8,128)(2,1)} %copy-done.8) | copy-start | bytes 16900
  140.3 26.8 %copy-start.15 = (f32[16]{0:T(128)S(1)}, f32[16]{0:T(128)}, u32[]{:S(2)}) copy-start(f32[16]{0:T(128)} %copy-done.14) | copy-start | bytes 196
  141.8 48.3 %copy-start.18 = (f32[16]{0:T(128)S(1)}, f32[16]{0:T(128)}, u32[]{:S(2)}) copy-start(f32[16]{0:T(128)} %get-tuple-element.16) | copy-start | bytes 196
Sparse Core Ops, SparseCore 0:
  9.6 14.8 all-gather.10
  26.0 13.1 all-gather.8
  40.8 13.1 all-gather.6
  90.6 11.2 reduce-scatter.7
  104.1 15.8 reduce-scatter.3
  122.1 15.0 reduce-scatter.5
